TPU v7x, 256 devices: a whole 4x4x8 slice. The times are simulated.
256 devices in a mesh: row: 16 (over x, z_lo, core), col: 16 (over y, z_hi).
Axes of the slice: x: 4, y: 4, z: 8 (z_hi: 4, z_lo: 2; z = z_hi * 2 + z_lo), core: 2. Of those that a mesh axis runs over, the one named last changes fastest.
Arguments:
- vectors: bfloat16 [2048, 1024], P(('row', 'col')), may hold values from -6 to 6
- block_values: bfloat16 [16, 16, 512, 4096], P('row', 'col'), may hold values from -0.09375 to 0.09375
- block_rows: int32 [16, 16, 512], P('row', 'col'), may hold values from 0 to 127, as said below
- block_cols: int32 [16, 16, 512], P('row', 'col'), may hold values from 0 to 127, as said below
- block_count: int32 [16, 16], P('row', 'col'), may hold values from 0 to 512, as said below
Outputs:
- product: float32 [2048, 1024], P(('row', 'col'))
Inputs may be any that keep to these rules, and one draw needn't show every extreme that they name: `block_rows`: in each tile the live slots name distinct positions with gi >= gj and come first, sorted by block row and then block column; slots past the count hold in-range indices that are not part of the matrix. `block_cols`: same slots as block_rows. `block_count`: some tile fills all 512 slots in every draw.
All inputs are finite; a program needn't handle non-finite values.
Results may differ from a plain program's by a relative error of at most 0.0003.
Values may be sent and summed in bfloat16 or wider, within the bound.
No kernel may reach another device: no remote copies, remote signals or barrier semaphores. Data moves between devices by JAX's collectives and lax.ppermute only.
A program may use at most 64 MiB of HBM per device.

v0:
```python
import jax
import jax.numpy as jnp
from jax import lax
from jax.sharding import PartitionSpec as P

NV = 16
BS = 64


def on_device(vectors, block_values, block_rows, block_cols, block_count):
    col_devices = lax.axis_size("col")
    row_index = lax.axis_index("row")
    col_index = lax.axis_index("col")
    piece_blocks = vectors.shape[0]
    width = vectors.shape[1]
    slot_count = block_rows.shape[2]
    matrices = block_values.reshape(slot_count, BS, BS)
    local_rows = block_rows.reshape(slot_count)
    local_cols = block_cols.reshape(slot_count)
    live_count = block_count.reshape(())
    row_segment = lax.all_gather(vectors, "col", axis=0, tiled=True)
    column_set = lax.all_gather(vectors, "row", axis=0, tiled=True)
    global_row = row_index * col_devices * piece_blocks + local_rows
    global_col = (
        local_cols // piece_blocks * col_devices + col_index
    ) * piece_blocks + local_cols % piece_blocks
    live = jnp.arange(slot_count, dtype=jnp.int32) < live_count
    weight = jnp.where(live, jnp.where(global_row == global_col, 0.5, 1.0), 0.0).astype(jnp.float32)
    col_vectors = jnp.take(column_set, local_cols, axis=0).reshape(slot_count, NV, BS)
    row_vectors = jnp.take(row_segment, local_rows, axis=0).reshape(slot_count, NV, BS)
    forward = jnp.einsum("nvk,nik->nvi", col_vectors, matrices, preferred_element_type=jnp.float32)
    backward = jnp.einsum("nvi,nik->nvk", row_vectors, matrices, preferred_element_type=jnp.float32)
    forward = (forward * weight[:, None, None]).reshape(slot_count, width)
    backward = (backward * weight[:, None, None]).reshape(slot_count, width)
    row_part = jax.ops.segment_sum(forward, local_rows, num_segments=row_segment.shape[0])
    col_part = jax.ops.segment_sum(backward, local_cols, num_segments=column_set.shape[0])
    whole_rows = lax.psum(row_part, "col")
    whole_cols = lax.psum(col_part, "row")
    mine_rows = lax.dynamic_slice_in_dim(whole_rows, col_index * piece_blocks, piece_blocks, 0)
    mine_cols = lax.dynamic_slice_in_dim(whole_cols, row_index * piece_blocks, piece_blocks, 0)
    return mine_rows + mine_cols


def solution(mesh):
    placed = (
        P(("row", "col"), None),
        P("row", "col", None, None),
        P("row", "col", None),
        P("row", "col", None),
        P("row", "col"),
    )
    return jax.shard_map(
        on_device, mesh=mesh, in_specs=placed, out_specs=P(("row", "col"), None), check_vma=False
    )
```

profile of v0, /device:TPU:1, one launch (start us, length us, event | category | flops | bytes accessed | tf_op | source)
XLA Modules:
  0.0 377.8 jit_solution(11786903282523296864)
XLA Ops:
  7.2 0.7 compare_and_fusion.1
  8.6 22.6 %all_gather.6 = bf16[128,1024]{1,0:T(8,128)(2,1)S(1)} all-gather(bf16[8,1024]{1,0:T(8,128)(2,1)} %param.7), channel_id=1, replica_groups=mesh['row'=16,'col'=16] {'row'}, dimensions={0}, use_global_device_ids=true | all-gather | bytes 278528 | tf_op jit(solution)/shard_map/all_gather | solution.py:22
  31.2 2.1 gather_fusion
  33.3 1.2 broadcast_select_fusion.1
  34.4 1.5 copy.6
  35.9 2.0 copy.8
  38.0 6.5 %copy.7 = bf16[1,1,512,4096]{2,3,1,0:T(8,128)(2,1)} copy(bf16[1,1,512,4096]{3,2,1,0:T(8,128)(2,1)} %param.8) | data formatting | bytes 8388608 | tf_op args[1]
  44.5 13.0 %copy.9 = bf16[512,64,64]{2,1,0:T(8,128)(2,1)} copy(bf16[512,64,64]{0,2,1:T(8,128)(2,1)} %bitcast.13) | data formatting | bytes 8388608 | tf_op jit(solution)/shard_map/reshape | solution.py:17
  57.5 9.8 %convolution_multiply_fusion.1 = f32[512,16,64]{2,1,0:T(8,128)} fusion(bf16[512,16,64]{2,1,0:T(8,128)(2,1)S(1)} %copy.8, bf16[512,64,64]{2,1,0:T(8,128)(2,1)} %copy.9, f32[512]{0:T(512)S(1)} %select_select_fusion), kind=kOutput, calls=%fused_computation.5 | convolution fusion | flops 67633152 | bytes 7342080 | tf_op jit(solution)/shard_map/nvk,nik->nvi/dot_general | solution.py:31
  67.3 2.8 copy.10
  70.2 1.9 copy.11
  72.0 6.5 %scatter_custom_fusion = f32[128,1024]{1,0:T(8,128)} fusion(s32[512]{0:T(512)S(1)} %bitcast.19, f32[512,1024]{1,0:T(8,128)} %copy.11, f32[]{:T(128)} %constant.47.clone.1), kind=kCustom, calls=%fused_computation.10 | custom fusion | flops 524288 | bytes 524800 | tf_op jit(solution)/shard_map/scatter-add | solution.py:35
  78.7 41.2 %all_gather.7 = bf16[128,1024]{1,0:T(8,128)(2,1)S(1)} all-gather(bf16[8,1024]{1,0:T(8,128)(2,1)S(1)} %copy-done), channel_id=1, replica_groups=mesh['row'=16,'col'=16] {'col'}, dimensions={0}, use_global_device_ids=true | all-gather | bytes 278528 | tf_op jit(solution)/shard_map/all_gather | solution.py:21
  119.8 2.1 gather_fusion.1
  121.9 1.2 broadcast_select_fusion
  123.1 1.5 copy.12
  124.6 2.0 copy.13
  126.7 7.7 %convolution_multiply_fusion = f32[512,16,64]{2,1,0:T(8,128)} fusion(bf16[512,16,64]{2,1,0:T(8,128)(2,1)S(1)} %copy.13, bf16[512,64,64]{2,1,0:T(8,128)(2,1)} %copy.9, f32[512]{0:T(512)S(1)} %select_select_fusion), kind=kOutput, calls=%fused_computation.4 | convolution fusion | flops 67633152 | bytes 7342080 | tf_op jit(solution)/shard_map/nvi,nik->nvk/dot_general | solution.py:32
  134.4 2.8 copy.15
  137.2 1.9 copy.16
  139.1 6.5 %scatter_custom_fusion.1 = f32[128,1024]{1,0:T(8,128)} fusion(s32[512]{0:T(512)S(1)} %bitcast.25, f32[512,1024]{1,0:T(8,128)} %copy.16, f32[]{:T(128)} %constant.47.clone.1), kind=kCustom, calls=%fused_computation.8 | custom fusion | flops 524288 | bytes 524800 | tf_op jit(solution)/shard_map/scatter-add | solution.py:36
  145.6 89.8 %all-reduce.3.cloned.1.call-done = f32[128,1024]{1,0:T(8,128)} async-done(((f32[128,1024]{1,0:T(8,128)}), f32[128,1024]{1,0:T(8,128)}) %all-reduce.3.cloned.1.call-update) | async-done | bytes 524304 | tf_op jit(solution)/shard_map/psum | solution.py:37
  235.3 134.3 %all-reduce.5.cloned.1.call-done = f32[128,1024]{1,0:T(8,128)} async-done(((f32[128,1024]{1,0:T(8,128)}), f32[128,1024]{1,0:T(8,128)}) %all-reduce.5.cloned.1.call-update) | async-done | bytes 524304 | tf_op jit(solution)/shard_map/psum | solution.py:38
  369.6 1.4 dynamic-slice_add_fusion
  (16 shorter events, 0.8 us)
Async XLA Ops:
  6.5 228.8 %all-reduce.3.cloned.1.call-start = ((), (), s32[]{:S(2)}) async-start(), calls=%async_computation | async-start | bytes 1048576 | tf_op jit(solution)/shard_map/psum | solution.py:37
  44.5 13.0 %copy-start.1 = (s32[1,1,512]{2,1,0:T(1,128)S(1)}, s32[1,1,512]{2,1,0:T(1,128)}, u32[]{:S(2)}) copy-start(s32[1,1,512]{2,1,0:T(1,128)} %param.9) | copy-start | bytes 6148
  44.5 13.0 %copy-start.2 = (s32[1,1,512]{2,1,0:T(1,128)S(1)}, s32[1,1,512]{2,1,0:T(1,128)}, u32[]{:S(2)}) copy-start(s32[1,1,512]{2,1,0:T(1,128)} %param.10) | copy-start | bytes 6148
  70.1 8.5 %copy-start = (bf16[8,1024]{1,0:T(8,128)(2,1)S(1)}, bf16[8,1024]{1,0:T(8,128)(2,1)}, u32[]{:S(2)}) copy-start(bf16[8,1024]{1,0:T(8,128)(2,1)} %param.7) | copy-start | bytes 49156
  78.6 291.0 %all-reduce.5.cloned.1.call-start = ((), (), s32[]{:S(2)}) async-start(), calls=%async_computation.1 | async-start | bytes 1048576 | tf_op jit(solution)/shard_map/psum | solution.py:38
Sparse Core Ops, SparseCore 0:
  78.7 156.5 all-reduce.2
  237.9 131.6 all-reduce.4
where the time goes:
time: 379 us; the launch traced here: 378 us
  waiting for transfers between devices  224 us (59%)
  blocking collectives  63.8 us (17%)
  local copies, waits for them, and re-layouts  40.1 us (11%)
  other arithmetic  18.2 us (5%)
  matrix products  17.5 us (5%)
  between operations  14.2 us (4%)
    psum x1, waiting for transfers between devices, on_device(): whole_cols = lax.psum(col_part, 'row')  134 us
    psum x1, waiting for transfers between devices, on_device(): whole_rows = lax.psum(row_part, 'col')  89.8 us
    all_gather x1, blocking collectives, on_device(): row_segment = lax.all_gather(vectors, 'col', axis=0, tiled=True)  41.2 us
    all_gather x1, blocking collectives, on_device(): column_set = lax.all_gather(vectors, 'row', axis=0, tiled=True)  22.6 us
    reshape x1, local copies, waits for them, and re-layouts, on_device(): matrices = block_values.reshape(slot_count, BS, BS)  13 us
    dot_general x1, matrix products, on_device(): jnp.einsum('nvk,nik->nvi', col_vectors, matrices, preferred_element_type=...  9.8 us
    dot_general x1, matrix products, on_device(): jnp.einsum('nvi,nik->nvk', row_vectors, matrices, preferred_element_type=...  7.68 us
  transfers between devices with their start and end apart: 2, of which 2 were waited for; matrix products, arithmetic and copies ran while one was open for 7% of the time, Pallas kernels for 0%

commit v1 on v0

--- a/solution.py
+++ b/solution.py
@@ -35,7 +35,7 @@
     row_part = jax.ops.segment_sum(forward, local_rows, num_segments=row_segment.shape[0])
     col_part = jax.ops.segment_sum(backward, local_cols, num_segments=column_set.shape[0])
     whole_rows = lax.psum(row_part, "col")
-    whole_cols = lax.psum(col_part, "row")
+    whole_cols = jnp.sum(lax.all_gather(col_part, "row"), 0)
     mine_rows = lax.dynamic_slice_in_dim(whole_rows, col_index * piece_blocks, piece_blocks, 0)
     mine_cols = lax.dynamic_slice_in_dim(whole_cols, row_index * piece_blocks, piece_blocks, 0)
     return mine_rows + mine_cols

time: 379 us -> 322 us (0.85)
  the two profiles are of different devices: /device:TPU:1 before, /device:TPU:2 now
where the time goes in v1:
time: 322 us
  waiting for transfers between devices  158 us (49%)
  blocking collectives  67.8 us (21%)
  local copies, waits for them, and re-layouts  40.1 us (12%)
  other arithmetic  22.4 us (7%)
  matrix products  17.5 us (5%)
  between operations  15.6 us (5%)
    psum x1, waiting for transfers between devices, on_device(): whole_rows = lax.psum(row_part, 'col')  157 us
    all_gather x1, blocking collectives, on_device(): row_segment = lax.all_gather(vectors, 'col', axis=0, tiled=True)  48.4 us
    all_gather x1, blocking collectives, on_device(): column_set = lax.all_gather(vectors, 'row', axis=0, tiled=True)  19.4 us
    reshape x1, local copies, waits for them, and re-layouts, on_device(): matrices = block_values.reshape(slot_count, BS, BS)  13 us
    dot_general x1, matrix products, on_device(): jnp.einsum('nvk,nik->nvi', col_vectors, matrices, preferred_element_type=...  9.91 us
    dot_general x1, matrix products, on_device(): jnp.einsum('nvi,nik->nvk', row_vectors, matrices, preferred_element_type=...  7.62 us
    scatter-add x1, other arithmetic, on_device(): jax.ops.segment_sum(forward, local_rows, num_segments=row_segment.shape[0])  6.58 us
    unnamed x7, local copies, waits for them, and re-layouts  6.49 us
  transfers between devices with their start and end apart: 2, of which 2 were waited for; matrix products, arithmetic and copies ran while one was open for 10% of the time, Pallas kernels for 0%

profile of v1, /device:TPU:2, one launch (start us, length us, event | category | flops | bytes accessed | tf_op | source)
XLA Modules:
  0.0 321.6 jit_solution(4255815016865871088)
XLA Ops:
  9.4 48.4 %all_gather.13 = bf16[128,1024]{1,0:T(8,128)(2,1)S(1)} all-gather(bf16[8,1024]{1,0:T(8,128)(2,1)} %param.7), channel_id=1, replica_groups=mesh['row'=16,'col'=16] {'col'}, dimensions={0}, use_global_device_ids=true | all-gather | bytes 278528 | tf_op jit(solution)/shard_map/all_gather | solution.py:21
  57.8 2.1 gather_fusion.1
  59.9 1.2 broadcast_select_fusion
  61.0 1.5 copy.12
  62.5 2.0 copy.13
  64.5 6.5 %copy.7 = bf16[1,1,512,4096]{2,3,1,0:T(8,128)(2,1)} copy(bf16[1,1,512,4096]{3,2,1,0:T(8,128)(2,1)} %param.8) | data formatting | bytes 8388608 | tf_op args[1]
  71.0 13.0 %copy.9 = bf16[512,64,64]{2,1,0:T(8,128)(2,1)} copy(bf16[512,64,64]{0,2,1:T(8,128)(2,1)} %bitcast.14) | data formatting | bytes 8388608 | tf_op jit(solution)/shard_map/reshape | solution.py:17
  84.0 7.6 %convolution_multiply_fusion = f32[512,16,64]{2,1,0:T(8,128)} fusion(bf16[512,16,64]{2,1,0:T(8,128)(2,1)S(1)} %copy.13, bf16[512,64,64]{2,1,0:T(8,128)(2,1)} %copy.9, f32[512]{0:T(512)S(1)} %select_select_fusion), kind=kOutput, calls=%fused_computation.4 | convolution fusion | flops 67633152 | bytes 7342080 | tf_op jit(solution)/shard_map/nvi,nik->nvk/dot_general | solution.py:32
  91.6 2.8 copy.15
  94.5 1.9 copy.16
  96.3 6.5 %scatter_custom_fusion.1 = f32[128,1024]{1,0:T(8,128)} fusion(s32[512]{0:T(512)S(1)} %bitcast.21, f32[512,1024]{1,0:T(8,128)} %copy.16, f32[]{:T(128)} %constant.47.clone.1), kind=kCustom, calls=%fused_computation.8 | custom fusion | flops 524288 | bytes 524800 | tf_op jit(solution)/shard_map/scatter-add | solution.py:36
  102.9 19.4 %all_gather.12 = bf16[128,1024]{1,0:T(8,128)(2,1)S(1)} all-gather(bf16[8,1024]{1,0:T(8,128)(2,1)S(1)} %copy-done), channel_id=1, replica_groups=mesh['row'=16,'col'=16] {'row'}, dimensions={0}, use_global_device_ids=true | all-gather | bytes 278528 | tf_op jit(solution)/shard_map/all_gather | solution.py:22
  122.3 2.0 gather_fusion
  124.4 1.2 broadcast_select_fusion.1
  125.6 1.5 copy.6
  127.1 2.0 copy.8
  129.1 9.9 %convolution_multiply_fusion.1 = f32[512,16,64]{2,1,0:T(8,128)} fusion(bf16[512,16,64]{2,1,0:T(8,128)(2,1)S(1)} %copy.8, bf16[512,64,64]{2,1,0:T(8,128)(2,1)} %copy.9, f32[512]{0:T(512)S(1)} %select_select_fusion), kind=kOutput, calls=%fused_computation.5 | convolution fusion | flops 67633152 | bytes 7342080 | tf_op jit(solution)/shard_map/nvk,nik->nvi/dot_general | solution.py:31
  139.0 2.9 copy.10
  141.9 1.9 copy.11
  143.8 6.6 %scatter_custom_fusion = f32[128,1024]{1,0:T(8,128)} fusion(s32[512]{0:T(512)S(1)} %bitcast.27, f32[512,1024]{1,0:T(8,128)} %copy.11, f32[]{:T(128)} %constant.47.clone.1), kind=kCustom, calls=%fused_computation.10 | custom fusion | flops 524288 | bytes 524800 | tf_op jit(solution)/shard_map/scatter-add | solution.py:35
  150.4 1.2 all-gather.3.cloned.1.call-done
  151.6 4.2 %reduce_sum.9 = f32[128,1024]{1,0:T(8,128)S(1)} reduce(f32[16,128,1024]{2,1,0:T(8,128)} %bitcast.17, f32[]{:T(128)} %constant.47.clone.1), dimensions={0}, to_apply=%region_3.5 | reduce | flops 1966080 | bytes 8912900 | tf_op jit(solution)/shard_map/reduce_sum | solution.py:38
  155.9 156.9 %all-reduce.2.cloned.1.call-done = f32[128,1024]{1,0:T(8,128)} async-done(((f32[128,1024]{1,0:T(8,128)}), f32[128,1024]{1,0:T(8,128)}) %all-reduce.2.cloned.1.call-update) | async-done | bytes 524304 | tf_op jit(solution)/shard_map/psum | solution.py:37
  312.7 1.4 dynamic-slice_add_fusion
  (17 shorter events, 1.5 us)
Async XLA Ops:
  7.4 144.3 %all-gather.3.cloned.1.call-start = ((), (), s32[]{:S(2)}) async-start(), calls=%async_computation.1 | async-start | bytes 8912896 | tf_op jit(solution)/shard_map/all_gather | solution.py:38
  71.0 13.0 %copy-start.1 = (s32[1,1,512]{2,1,0:T(1,128)S(1)}, s32[1,1,512]{2,1,0:T(1,128)}, u32[]{:S(2)}) copy-start(s32[1,1,512]{2,1,0:T(1,128)} %param.10) | copy-start | bytes 6148
  71.0 13.0 %copy-start.2 = (s32[1,1,512]{2,1,0:T(1,128)S(1)}, s32[1,1,512]{2,1,0:T(1,128)}, u32[]{:S(2)}) copy-start(s32[1,1,512]{2,1,0:T(1,128)} %param.9) | copy-start | bytes 6148
  94.5 8.5 %copy-start = (bf16[8,1024]{1,0:T(8,128)(2,1)S(1)}, bf16[8,1024]{1,0:T(8,128)(2,1)}, u32[]{:S(2)}) copy-start(bf16[8,1024]{1,0:T(8,128)(2,1)} %param.7) | copy-start | bytes 49156
  102.8 209.9 %all-reduce.2.cloned.1.call-start = ((), (), s32[]{:S(2)}) async-start(), calls=%async_computation | async-start | bytes 1048576 | tf_op jit(solution)/shard_map/psum | solution.py:37
Sparse Core Ops, SparseCore 0:
  103.0 48.6 all-gather.2
Sparse Core Ops, SparseCore 1:
  150.5 162.2 all-reduce.1
